TPU v7x, 256 devices: a whole 4x4x8 slice. The times are simulated.
256 devices in a mesh: illum: 16 (over z_hi, x), row: 4 (over y), col: 4 (over z_lo, core).
Axes of the slice: x: 4, y: 4, z: 8 (z_hi: 4, z_lo: 2; z = z_hi * 2 + z_lo), core: 2. Of those that a mesh axis runs over, the one named last changes fastest.
Arguments:
- phase_delay: float32 [2, 512, 4096], P(None, ('row', 'illum'), 'col'), may hold values from -1 to 1
- angles: int32 [16, 2], P('illum'), may hold values from -8 to 8
- measured: bfloat16 [2, 16, 512, 4096], P(None, 'illum', 'row', 'col'), may hold values from -120 to 120, as said below
Outputs:
- phase_grad: float32 [2, 512, 4096], P(None, ('row', 'illum'), 'col')
Inputs may be any that keep to these rules, and one draw needn't show every extreme that they name: Real and imaginary parts of a measured field, with scales that vary over rows and columns.
All inputs are finite; a program needn't handle non-finite values.
Results may differ from a plain program's by a relative error of at most 0.0003.
Values sent between devices are 32-bit elements; how exact they have to be, the bound alone decides.
A program may use at most 64 MiB of HBM per device.

v0:
```python
import math
import jax
import jax.numpy as jnp
from jax import lax
from jax.sharding import PartitionSpec as P

SWEEPS = 2
beta_step = 0.5
eps_energy = 1e-06


def with_halo(x, sides, width):
    for axis, dim in sides:
        peers, length = (lax.axis_size(axis), x.shape[dim])
        up = [(i, (i + 1) % peers) for i in range(peers - 1)]
        down = [(j, i) for i, j in up]
        last = lax.slice_in_dim(x, length - width, length, axis=dim)
        first = lax.slice_in_dim(x, 0, width, axis=dim)
        before = lax.ppermute(last, axis, up)
        after = lax.ppermute(first, axis, down)
        x = jnp.concatenate([before, x, after], axis=dim)
    return x


def neighbour_sum(padded):
    return (
        padded[..., 2:, 1:-1]
        + padded[..., :-2, 1:-1]
        + padded[..., 1:-1, 2:]
        + padded[..., 1:-1, :-2]
    )


def exchange_rims(wave_field):
    return with_halo(wave_field, (("row", 2), ("col", 3)), 1)


def propagate(wave_field, direction):
    beta_sign = direction * beta_step
    divisor = 1.0 + 16.0 * beta_sign * beta_sign
    beside_all = neighbour_sum(exchange_rims(wave_field))
    real_part, imag_part = (wave_field[0], wave_field[1])
    rhs_real = real_part + 4.0 * beta_sign * imag_part - beta_sign * beside_all[1]
    rhs_imag = imag_part - 4.0 * beta_sign * real_part + beta_sign * beside_all[0]
    for sweep in range(SWEEPS):
        if sweep > 0:
            beside_all = neighbour_sum(exchange_rims(jnp.stack([real_part, imag_part])))
        total_real = rhs_real - beta_sign * beside_all[1]
        total_imag = rhs_imag + beta_sign * beside_all[0]
        real_part = (total_real + 4.0 * beta_sign * total_imag) / divisor
        imag_part = (total_imag - 4.0 * beta_sign * total_real) / divisor
    return jnp.stack([real_part, imag_part])


def per_device(phase_delay, angles, measured):
    illum_count = lax.axis_size("illum")
    stripe = phase_delay.shape[1]
    rows_tile = stripe * illum_count
    cols_tile = measured.shape[3]
    total_rows = rows_tile * lax.axis_size("row")
    total_cols = cols_tile * lax.axis_size("col")
    row_ids = lax.axis_index("row") * rows_tile + lax.iota(jnp.int32, rows_tile)
    col_ids = lax.axis_index("col") * cols_tile + lax.iota(jnp.int32, cols_tile)

    def advance(field_now, direction):
        return propagate(field_now, direction)

    along_x = angles[:, 0:1] * row_ids[None, :] % total_rows
    along_y = angles[:, 1:2] * col_ids[None, :] % total_cols
    angle_phase = (
        2.0
        * math.pi
        * (
            along_x.astype(jnp.float32)[:, :, None] / total_rows
            + along_y.astype(jnp.float32)[:, None, :] / total_cols
        )
    )
    wave_field = jnp.stack([jnp.cos(angle_phase), jnp.sin(angle_phase)])
    target = measured.astype(jnp.float32)
    energy = (
        lax.psum(jnp.sum(target * target, axis=(0, 2, 3)), ("row", "col"))
        / (total_rows * total_cols)
        + eps_energy
    )
    all_planes = lax.all_gather(phase_delay, "illum", axis=1, tiled=True)
    stored = []
    for depth_index in range(phase_delay.shape[0]):
        phase_plane = all_planes[depth_index]
        cosine = jnp.cos(phase_plane)
        sine_part = jnp.sin(phase_plane)
        modulated = jnp.stack(
            [
                wave_field[0] * cosine - wave_field[1] * sine_part,
                wave_field[0] * sine_part + wave_field[1] * cosine,
            ]
        )
        stored.append((modulated, cosine, sine_part))
        wave_field = advance(modulated, 1.0)
    adjoint_wave = 2.0 * (wave_field - target) / energy[None, :, None, None]
    slice_grads = [None] * len(stored)
    for depth_index in reversed(range(len(stored))):
        modulated, cosine, sine_part = stored[depth_index]
        adjoint_wave = advance(adjoint_wave, -1.0)
        slice_grads[depth_index] = jnp.sum(
            adjoint_wave[1] * modulated[0] - adjoint_wave[0] * modulated[1], axis=0
        )
        if depth_index > 0:
            adjoint_wave = jnp.stack(
                [
                    adjoint_wave[0] * cosine + adjoint_wave[1] * sine_part,
                    adjoint_wave[1] * cosine - adjoint_wave[0] * sine_part,
                ]
            )
    local_grads = jnp.stack(slice_grads)
    summed = lax.psum(local_grads, "illum")
    return lax.dynamic_slice_in_dim(summed, lax.axis_index("illum") * stripe, stripe, 1)


def solution(mesh):
    placed = (P(None, ("row", "illum"), "col"), P("illum", None), P(None, "illum", "row", "col"))
    return jax.shard_map(
        per_device,
        mesh=mesh,
        in_specs=placed,
        out_specs=P(None, ("row", "illum"), "col"),
        check_vma=False,
    )
```

profile of v0, /device:TPU:2, one launch (start us, length us, event | category | flops | bytes accessed | tf_op | source)
XLA Modules:
  0.0 428.9 jit_solution(10566999443613107633)
XLA Ops:
  6.5 0.7 all-gather.2.cloned.1.call-update
  9.8 55.3 %all-gather.2.cloned.1.call-done = f32[2,128,1024]{2,1,0:T(8,128)} async-done(((f32[2,8,1024]{2,1,0:T(8,128)}), f32[2,128,1024]{2,1,0:T(8,128)}) %all-gather.2.cloned.1.call-update) | async-done | bytes 1048592 | tf_op jit(solution)/shard_map/all_gather | solution.py:85
  65.1 4.8 %fusion.64 = (f32[1,1,128,1024]{3,2,1,0:T(8,128)S(1)}, f32[1,1,128,1024]{3,2,1,0:T(8,128)S(1)}) fusion(f32[2,128,1024]{2,1,0:T(8,128)} %all-gather.2.cloned.1.call-done, f32[1024]{0:T(1024)S(1)} %fusion.60, f32[128]{0:T(128)S(1)} %fusion.62), kind=kLoop, calls=%fused_computation.267 | loop fusion | flops 1048576 | bytes 1577472 | tf_op jit(solution)/shard_map/stack | solution.py:91
  70.0 3.4 collective-permute-start.1
  73.4 1.3 collective-permute-start
  74.7 4.2 collective-permute-done
  79.0 1.3 collective-permute-start.2
  80.3 3.2 collective-permute-start.3
  83.5 1.0 collective-permute-done.3
  85.2 4.2 multiply_bitcast_fusion.7
  89.4 3.4 collective-permute-start.5
  92.8 1.3 collective-permute-start.4
  94.2 4.2 collective-permute-done.4
  98.5 1.3 collective-permute-start.6
  99.8 3.0 collective-permute-start.7
  102.9 1.0 collective-permute-done.7
  103.8 0.7 fusion.21
  104.5 6.1 %multiply_subtract_fusion.3 = (f32[1,128,1024]{2,1,0:T(8,128)S(1)}, f32[1,128,1024]{2,1,0:T(8,128)S(1)}) fusion(f32[2,128,1024]{2,1,0:T(8,128)S(1)} %copy-done, f32[2,1,128,1024]{3,2,1,0:T(8,128)S(1)} %fusion.21, f32[2,1,128,1024]{3,2,1,0:T(8,128)S(1)} %fusion.24, f32[1024]{0:T(1024)S(1)} %fusion.60, f32[128]{0:T(128)S(1)} %fusion.62), kind=kLoop, calls=%fused_computation.187 | loop fusion | flops 4194304 | bytes 4198912 | tf_op jit(solution)/shard_map/sub | solution.py:93
  110.6 3.1 collective-permute-start.9
  113.7 1.3 collective-permute-start.8
  115.1 4.2 collective-permute-done.8
  119.4 1.3 collective-permute-start.10
  120.7 5.5 %collective-permute-start.11 = (f32[2,1,130,1]{3,2,1,0:T(8,128)S(1)}, f32[2,1,130,1]{3,2,1,0:T(8,128)S(1)}, u32[]{:S(2)}, u32[]{:S(2)}) collective-permute-start(f32[2,1,130,1]{3,2,1,0:T(8,128)S(1)} %get-tuple-element.33), channel_id=1, source_target_pairs={{0,1},{1,2},{2,3},{4,5},{5,6},{6,7},{8,9},{9,10},{10,11},{12,13},{... | collective-permute-start | bytes 3128 | tf_op jit(solution)/shard_map/ppermute | solution.py:19
  126.2 1.0 collective-permute-done.11
  129.1 2.2 collective-permute-start.13
  131.3 1.4 collective-permute-start.12
  132.8 4.2 collective-permute-done.12
  137.0 0.8 pad_maximum_fusion.111
  137.8 1.3 collective-permute-start.14
  139.1 5.7 %collective-permute-start.15 = (f32[2,1,130,1]{3,2,1,0:T(8,128)}, f32[2,1,130,1]{3,2,1,0:T(8,128)S(1)}, u32[]{:S(2)}, u32[]{:S(2)}) collective-permute-start(f32[2,1,130,1]{3,2,1,0:T(8,128)} %get-tuple-element.31), channel_id=1, source_target_pairs={{0,1},{1,2},{2,3},{4,5},{5,6},{6,7},{8,9},{9,10},{10,11},{12,13},{... | collective-permute-start | bytes 3128 | tf_op jit(solution)/shard_map/ppermute | solution.py:19
  144.9 0.9 fusion.2
  145.7 31.6 %psum.14 = f32[1]{0:T(128)} all-reduce(f32[1]{0:T(128)} %bitcast.20), channel_id=1, replica_groups=mesh['illum'=16,'row'=4,'col'=4] {'row','col'}, use_global_device_ids=true, to_apply=%region_1.2 | all-reduce | flops 1 | bytes 8 | tf_op jit(solution)/shard_map/psum | solution.py:81
  178.1 0.7 fusion.15
  179.4 0.8 copy-done.6
  180.5 1.3 collective-permute-start.17
  181.8 1.3 collective-permute-start.16
  183.1 4.2 collective-permute-done.16
  187.4 1.3 collective-permute-start.18
  188.7 3.0 collective-permute-start.19
  191.8 1.0 collective-permute-done.19
  193.8 1.6 collective-permute-start.21
  195.4 1.3 collective-permute-start.20
  196.8 4.2 collective-permute-done.20
  201.1 1.3 collective-permute-start.22
  202.4 3.2 collective-permute-start.23
  205.6 0.8 collective-permute-done.23
  207.1 2.3 multiply_add_fusion
  209.4 2.1 multiply_subtract_fusion.2
  211.5 1.9 collective-permute-start.25
  213.5 1.3 collective-permute-start.24
  214.8 4.2 collective-permute-done.24
  219.1 1.3 collective-permute-start.26
  220.4 5.2 %collective-permute-start.27 = (f32[2,1,130,1]{3,2,1,0:T(8,128)S(1)}, f32[2,1,130,1]{3,2,1,0:T(8,128)S(1)}, u32[]{:S(2)}, u32[]{:S(2)}) collective-permute-start(f32[2,1,130,1]{3,2,1,0:T(8,128)S(1)} %get-tuple-element.25), channel_id=1, source_target_pairs={{0,1},{1,2},{2,3},{4,5},{5,6},{6,7},{8,9},{9,10},{10,11},{12,13},{... | collective-permute-start | bytes 3128 | tf_op jit(solution)/shard_map/ppermute | solution.py:19
  225.7 1.0 collective-permute-done.27
  227.9 2.2 collective-permute-start.29
  230.1 1.3 collective-permute-start.28
  231.5 4.2 collective-permute-done.28
  235.8 1.3 collective-permute-start.30
  237.1 5.7 %collective-permute-start.31 = (f32[2,1,130,1]{3,2,1,0:T(8,128)S(1)}, f32[2,1,130,1]{3,2,1,0:T(8,128)S(1)}, u32[]{:S(2)}, u32[]{:S(2)}) collective-permute-start(f32[2,1,130,1]{3,2,1,0:T(8,128)S(1)} %get-tuple-element.23), channel_id=1, source_target_pairs={{0,1},{1,2},{2,3},{4,5},{5,6},{6,7},{8,9},{9,10},{10,11},{12,13},{... | collective-permute-start | bytes 3128 | tf_op jit(solution)/shard_map/ppermute | solution.py:19
  242.9 1.0 collective-permute-done.31
  244.5 4.1 multiply_subtract_fusion.1
  248.7 1.1 pad_maximum_fusion.92
  249.7 170.8 %all-reduce.2.cloned.1.call-done = f32[2,128,1024]{2,1,0:T(8,128)} async-done(((f32[2,128,1024]{2,1,0:T(8,128)}), f32[2,128,1024]{2,1,0:T(8,128)}) %all-reduce.2.cloned.1.call-update) | async-done | bytes 1048592 | tf_op jit(solution)/shard_map/psum | solution.py:115
  420.5 1.5 constant_dynamic-slice_fusion
  (66 shorter events, 10.9 us)
Async XLA Ops:
  6.5 58.6 %all-gather.2.cloned.1.call-start = ((), (), s32[]{:S(2)}) async-start(), calls=%async_computation | async-start | bytes 1114112 | tf_op jit(solution)/shard_map/all_gather | solution.py:85
  7.3 413.3 %all-reduce.2.cloned.1.call-start = ((), (), s32[]{:S(2)}) async-start(), calls=%async_computation.1 | async-start | bytes 2097152 | tf_op jit(solution)/shard_map/psum | solution.py:115
  7.3 0.7 copy-start.7
  70.0 4.7 %collective-permute-start.1 = (f32[2,1,1,1024]{3,2,1,0:T(1,128)S(1)}, f32[2,1,1,1024]{3,2,1,0:T(1,128)S(1)}, u32[]{:S(2)}, u32[]{:S(2)}) collective-permute-start(f32[2,1,1,1024]{3,2,1,0:T(1,128)S(1)} %get-tuple-element.56), channel_id=1, source_target_pairs={{0,4},{4,8},{8,12},{1,5},{5,9},{9,13},{2,6},{6,10},{10,14},{3,7},{... | collective-permute-start | bytes 24584 | tf_op jit(solution)/shard_map/ppermute | solution.py:19
  73.4 5.5 %collective-permute-start = (f32[2,1,1,1024]{3,2,1,0:T(1,128)S(1)}, f32[2,1,1,1024]{3,2,1,0:T(1,128)S(1)}, u32[]{:S(2)}, u32[]{:S(2)}) collective-permute-start(f32[2,1,1,1024]{3,2,1,0:T(1,128)S(1)} %get-tuple-element.57), channel_id=1, source_target_pairs={{4,0},{8,4},{12,8},{5,1},{9,5},{13,9},{6,2},{10,6},{14,10},{7,3},{... | collective-permute-start | bytes 24584 | tf_op jit(solution)/shard_map/ppermute | solution.py:20
  79.0 4.5 %collective-permute-start.2 = (f32[2,1,130,1]{3,2,1,0:T(8,128)S(1)}, f32[2,1,130,1]{3,2,1,0:T(8,128)S(1)}, u32[]{:S(2)}, u32[]{:S(2)}) collective-permute-start(f32[2,1,130,1]{3,2,1,0:T(8,128)S(1)} %get-tuple-element.36), channel_id=1, source_target_pairs={{1,0},{2,1},{3,2},{5,4},{6,5},{7,6},{9,8},{10,9},{11,10},{13,12},{... | collective-permute-start | bytes 3128 | tf_op jit(solution)/shard_map/ppermute | solution.py:20
  80.3 4.8 %copy-start = (f32[2,128,1024]{2,1,0:T(8,128)S(1)}, f32[2,128,1024]{2,1,0:T(8,128)}, u32[]{:S(2)}) copy-start(f32[2,128,1024]{2,1,0:T(8,128)} %all-gather.2.cloned.1.call-done) | copy-start | bytes 3145732
  80.3 4.1 collective-permute-start.3
  89.4 4.8 %collective-permute-start.5 = (f32[2,1,1,1024]{3,2,1,0:T(1,128)S(1)}, f32[2,1,1,1024]{3,2,1,0:T(1,128)S(1)}, u32[]{:S(2)}, u32[]{:S(2)}) collective-permute-start(f32[2,1,1,1024]{3,2,1,0:T(1,128)S(1)} %get-tuple-element.54), channel_id=1, source_target_pairs={{0,4},{4,8},{8,12},{1,5},{5,9},{9,13},{2,6},{6,10},{10,14},{3,7},{... | collective-permute-start | bytes 24584 | tf_op jit(solution)/shard_map/ppermute | solution.py:19
  92.8 5.5 %collective-permute-start.4 = (f32[2,1,1,1024]{3,2,1,0:T(1,128)S(1)}, f32[2,1,1,1024]{3,2,1,0:T(1,128)S(1)}, u32[]{:S(2)}, u32[]{:S(2)}) collective-permute-start(f32[2,1,1,1024]{3,2,1,0:T(1,128)S(1)} %get-tuple-element.55), channel_id=1, source_target_pairs={{4,0},{8,4},{12,8},{5,1},{9,5},{13,9},{6,2},{10,6},{14,10},{7,3},{... | collective-permute-start | bytes 24584 | tf_op jit(solution)/shard_map/ppermute | solution.py:20
  98.5 4.3 %collective-permute-start.6 = (f32[2,1,130,1]{3,2,1,0:T(8,128)S(1)}, f32[2,1,130,1]{3,2,1,0:T(8,128)S(1)}, u32[]{:S(2)}, u32[]{:S(2)}) collective-permute-start(f32[2,1,130,1]{3,2,1,0:T(8,128)S(1)} %get-tuple-element.34), channel_id=1, source_target_pairs={{1,0},{2,1},{3,2},{5,4},{6,5},{7,6},{9,8},{10,9},{11,10},{13,12},{... | collective-permute-start | bytes 3128 | tf_op jit(solution)/shard_map/ppermute | solution.py:20
  99.8 4.0 collective-permute-start.7
  110.6 4.5 %collective-permute-start.9 = (f32[2,1,1,1024]{3,2,1,0:T(1,128)S(1)}, f32[2,1,1,1024]{3,2,1,0:T(1,128)S(1)}, u32[]{:S(2)}, u32[]{:S(2)}) collective-permute-start(f32[2,1,1,1024]{3,2,1,0:T(1,128)S(1)} %get-tuple-element.52), channel_id=1, source_target_pairs={{0,4},{4,8},{8,12},{1,5},{5,9},{9,13},{2,6},{6,10},{10,14},{3,7},{... | collective-permute-start | bytes 24584 | tf_op jit(solution)/shard_map/ppermute | solution.py:19
  113.7 5.5 %collective-permute-start.8 = (f32[2,1,1,1024]{3,2,1,0:T(1,128)S(1)}, f32[2,1,1,1024]{3,2,1,0:T(1,128)S(1)}, u32[]{:S(2)}, u32[]{:S(2)}) collective-permute-start(f32[2,1,1,1024]{3,2,1,0:T(1,128)S(1)} %get-tuple-element.53), channel_id=1, source_target_pairs={{4,0},{8,4},{12,8},{5,1},{9,5},{13,9},{6,2},{10,6},{14,10},{7,3},{... | collective-permute-start | bytes 24584 | tf_op jit(solution)/shard_map/ppermute | solution.py:20
  119.4 6.8 %collective-permute-start.10 = (f32[2,1,130,1]{3,2,1,0:T(8,128)S(1)}, f32[2,1,130,1]{3,2,1,0:T(8,128)S(1)}, u32[]{:S(2)}, u32[]{:S(2)}) collective-permute-start(f32[2,1,130,1]{3,2,1,0:T(8,128)S(1)} %get-tuple-element.32), channel_id=1, source_target_pairs={{1,0},{2,1},{3,2},{5,4},{6,5},{7,6},{9,8},{10,9},{11,10},{13,12},{... | collective-permute-start | bytes 3128 | tf_op jit(solution)/shard_map/ppermute | solution.py:20
  120.7 6.4 %collective-permute-start.11 = (f32[2,1,130,1]{3,2,1,0:T(8,128)S(1)}, f32[2,1,130,1]{3,2,1,0:T(8,128)S(1)}, u32[]{:S(2)}, u32[]{:S(2)}) collective-permute-start(f32[2,1,130,1]{3,2,1,0:T(8,128)S(1)} %get-tuple-element.33), channel_id=1, source_target_pairs={{0,1},{1,2},{2,3},{4,5},{5,6},{6,7},{8,9},{9,10},{10,11},{12,13},{... | collective-permute-start | bytes 3128 | tf_op jit(solution)/shard_map/ppermute | solution.py:19
  128.1 0.8 copy-start.1
  128.1 1.0 copy-start.3
  129.1 3.7 collective-permute-start.13
  131.3 13.5 %copy-start.5 = (bf16[2,1,128,1024]{3,2,1,0:T(8,128)(2,1)S(1)}, bf16[2,1,128,1024]{3,2,1,0:T(8,128)(2,1)}, u32[]{:S(2)}) copy-start(bf16[2,1,128,1024]{3,2,1,0:T(8,128)(2,1)} %param.5) | copy-start | bytes 1572868
  131.3 5.7 %collective-permute-start.12 = (f32[2,1,1,1024]{3,2,1,0:T(1,128)S(1)}, f32[2,1,1,1024]{3,2,1,0:T(1,128)S(1)}, u32[]{:S(2)}, u32[]{:S(2)}) collective-permute-start(f32[2,1,1,1024]{3,2,1,0:T(1,128)S(1)} %get-tuple-element.51), channel_id=1, source_target_pairs={{4,0},{8,4},{12,8},{5,1},{9,5},{13,9},{6,2},{10,6},{14,10},{7,3},{... | collective-permute-start | bytes 24584 | tf_op jit(solution)/shard_map/ppermute | solution.py:20
  137.8 40.2 %collective-permute-start.14 = (f32[2,1,130,1]{3,2,1,0:T(8,128)}, f32[2,1,130,1]{3,2,1,0:T(8,128)S(1)}, u32[]{:S(2)}, u32[]{:S(2)}) collective-permute-start(f32[2,1,130,1]{3,2,1,0:T(8,128)} %get-tuple-element.30), channel_id=1, source_target_pairs={{1,0},{2,1},{3,2},{5,4},{6,5},{7,6},{9,8},{10,9},{11,10},{13,12},{... | collective-permute-start | bytes 3128 | tf_op jit(solution)/shard_map/ppermute | solution.py:20
  139.1 38.9 %collective-permute-start.15 = (f32[2,1,130,1]{3,2,1,0:T(8,128)}, f32[2,1,130,1]{3,2,1,0:T(8,128)S(1)}, u32[]{:S(2)}, u32[]{:S(2)}) collective-permute-start(f32[2,1,130,1]{3,2,1,0:T(8,128)} %get-tuple-element.31), channel_id=1, source_target_pairs={{0,1},{1,2},{2,3},{4,5},{5,6},{6,7},{8,9},{9,10},{10,11},{12,13},{... | collective-permute-start | bytes 3128 | tf_op jit(solution)/shard_map/ppermute | solution.py:19
  178.0 1.0 copy-start.2
  178.0 1.2 copy-start.4
  179.2 1.0 copy-start.6
  180.5 2.6 collective-permute-start.17
  181.8 5.5 %collective-permute-start.16 = (f32[2,1,1,1024]{3,2,1,0:T(1,128)S(1)}, f32[2,1,1,1024]{3,2,1,0:T(1,128)S(1)}, u32[]{:S(2)}, u32[]{:S(2)}) collective-permute-start(f32[2,1,1,1024]{3,2,1,0:T(1,128)S(1)} %get-tuple-element.49), channel_id=1, source_target_pairs={{4,0},{8,4},{12,8},{5,1},{9,5},{13,9},{6,2},{10,6},{14,10},{7,3},{... | collective-permute-start | bytes 24584 | tf_op jit(solution)/shard_map/ppermute | solution.py:20
  187.4 4.3 %collective-permute-start.18 = (f32[2,1,130,1]{3,2,1,0:T(8,128)S(1)}, f32[2,1,130,1]{3,2,1,0:T(8,128)S(1)}, u32[]{:S(2)}, u32[]{:S(2)}) collective-permute-start(f32[2,1,130,1]{3,2,1,0:T(8,128)S(1)} %get-tuple-element.28), channel_id=1, source_target_pairs={{1,0},{2,1},{3,2},{5,4},{6,5},{7,6},{9,8},{10,9},{11,10},{13,12},{... | collective-permute-start | bytes 3128 | tf_op jit(solution)/shard_map/ppermute | solution.py:20
  188.7 4.0 collective-permute-start.19
  193.8 3.0 collective-permute-start.21
  195.4 5.5 %collective-permute-start.20 = (f32[2,1,1,1024]{3,2,1,0:T(1,128)S(1)}, f32[2,1,1,1024]{3,2,1,0:T(1,128)S(1)}, u32[]{:S(2)}, u32[]{:S(2)}) collective-permute-start(f32[2,1,1,1024]{3,2,1,0:T(1,128)S(1)} %get-tuple-element.47), channel_id=1, source_target_pairs={{4,0},{8,4},{12,8},{5,1},{9,5},{13,9},{6,2},{10,6},{14,10},{7,3},{... | collective-permute-start | bytes 24584 | tf_op jit(solution)/shard_map/ppermute | solution.py:20
  201.1 4.5 %collective-permute-start.22 = (f32[2,1,130,1]{3,2,1,0:T(8,128)S(1)}, f32[2,1,130,1]{3,2,1,0:T(8,128)S(1)}, u32[]{:S(2)}, u32[]{:S(2)}) collective-permute-start(f32[2,1,130,1]{3,2,1,0:T(8,128)S(1)} %get-tuple-element.26), channel_id=1, source_target_pairs={{1,0},{2,1},{3,2},{5,4},{6,5},{7,6},{9,8},{10,9},{11,10},{13,12},{... | collective-permute-start | bytes 3128 | tf_op jit(solution)/shard_map/ppermute | solution.py:20
  202.4 4.0 collective-permute-start.23
  211.5 3.3 collective-permute-start.25
  213.5 5.5 %collective-permute-start.24 = (f32[2,1,1,1024]{3,2,1,0:T(1,128)S(1)}, f32[2,1,1,1024]{3,2,1,0:T(1,128)S(1)}, u32[]{:S(2)}, u32[]{:S(2)}) collective-permute-start(f32[2,1,1,1024]{3,2,1,0:T(1,128)S(1)} %get-tuple-element.43), channel_id=1, source_target_pairs={{4,0},{8,4},{12,8},{5,1},{9,5},{13,9},{6,2},{10,6},{14,10},{7,3},{... | collective-permute-start | bytes 24584 | tf_op jit(solution)/shard_map/ppermute | solution.py:20
  219.1 6.5 %collective-permute-start.26 = (f32[2,1,130,1]{3,2,1,0:T(8,128)S(1)}, f32[2,1,130,1]{3,2,1,0:T(8,128)S(1)}, u32[]{:S(2)}, u32[]{:S(2)}) collective-permute-start(f32[2,1,130,1]{3,2,1,0:T(8,128)S(1)} %get-tuple-element.24), channel_id=1, source_target_pairs={{1,0},{2,1},{3,2},{5,4},{6,5},{7,6},{9,8},{10,9},{11,10},{13,12},{... | collective-permute-start | bytes 3128 | tf_op jit(solution)/shard_map/ppermute | solution.py:20
  220.4 6.2 %collective-permute-start.27 = (f32[2,1,130,1]{3,2,1,0:T(8,128)S(1)}, f32[2,1,130,1]{3,2,1,0:T(8,128)S(1)}, u32[]{:S(2)}, u32[]{:S(2)}) collective-permute-start(f32[2,1,130,1]{3,2,1,0:T(8,128)S(1)} %get-tuple-element.25), channel_id=1, source_target_pairs={{0,1},{1,2},{2,3},{4,5},{5,6},{6,7},{8,9},{9,10},{10,11},{12,13},{... | collective-permute-start | bytes 3128 | tf_op jit(solution)/shard_map/ppermute | solution.py:19
  227.9 3.6 collective-permute-start.29
  230.1 5.5 %collective-permute-start.28 = (f32[2,1,1,1024]{3,2,1,0:T(1,128)S(1)}, f32[2,1,1,1024]{3,2,1,0:T(1,128)S(1)}, u32[]{:S(2)}, u32[]{:S(2)}) collective-permute-start(f32[2,1,1,1024]{3,2,1,0:T(1,128)S(1)} %get-tuple-element.41), channel_id=1, source_target_pairs={{4,0},{8,4},{12,8},{5,1},{9,5},{13,9},{6,2},{10,6},{14,10},{7,3},{... | collective-permute-start | bytes 24584 | tf_op jit(solution)/shard_map/ppermute | solution.py:20
  235.8 7.1 %collective-permute-start.30 = (f32[2,1,130,1]{3,2,1,0:T(8,128)S(1)}, f32[2,1,130,1]{3,2,1,0:T(8,128)S(1)}, u32[]{:S(2)}, u32[]{:S(2)}) collective-permute-start(f32[2,1,130,1]{3,2,1,0:T(8,128)S(1)} %get-tuple-element.22), channel_id=1, source_target_pairs={{1,0},{2,1},{3,2},{5,4},{6,5},{7,6},{9,8},{10,9},{11,10},{13,12},{... | collective-permute-start | bytes 3128 | tf_op jit(solution)/shard_map/ppermute | solution.py:20
  237.1 6.7 %collective-permute-start.31 = (f32[2,1,130,1]{3,2,1,0:T(8,128)S(1)}, f32[2,1,130,1]{3,2,1,0:T(8,128)S(1)}, u32[]{:S(2)}, u32[]{:S(2)}) collective-permute-start(f32[2,1,130,1]{3,2,1,0:T(8,128)S(1)} %get-tuple-element.23), channel_id=1, source_target_pairs={{0,1},{1,2},{2,3},{4,5},{5,6},{6,7},{8,9},{9,10},{10,11},{12,13},{... | collective-permute-start | bytes 3128 | tf_op jit(solution)/shard_map/ppermute | solution.py:19
Sparse Core Ops, SparseCore 0:
  9.8 55.2 all-gather.1
  249.9 170.6 all-reduce.1
where the time goes:
time: 430 us; the launch traced here: 429 us
  waiting for transfers between devices  267 us (62%)
  starting transfers between devices  74.6 us (17%)
  other arithmetic  35.7 us (8%)
  blocking collectives  31.6 us (7%)
  between operations  14.8 us (3%)
  local copies, waits for them, and re-layouts  4.82 us (1%)
    psum x1, waiting for transfers between devices, per_device(): summed = lax.psum(local_grads, 'illum')  171 us
    all_gather x1, waiting for transfers between devices, per_device(): all_planes = lax.all_gather(phase_delay, 'illum', axis=1, tiled=True)  55.3 us
    ppermute x16, starting transfers between devices, with_halo(): before = lax.ppermute(last, axis, up)  53.8 us
    ppermute x16, waiting for transfers between devices, with_halo(): after = lax.ppermute(first, axis, down)  33.6 us
    psum x1, blocking collectives, per_device(): lax.psum(jnp.sum(target * target, axis=(0, 2, 3)), ('row', 'col'))  31.6 us
    ppermute x16, starting transfers between devices, with_halo(): after = lax.ppermute(first, axis, down)  20.8 us
  transfers between devices with their start and end apart: 34, of which 17 were waited for; matrix products, arithmetic and copies ran while one was open for 1% of the time, Pallas kernels for 0%

commit v1 on v0

--- a/solution.py
+++ b/solution.py
@@ -82,7 +82,9 @@
         / (total_rows * total_cols)
         + eps_energy
     )
-    all_planes = lax.all_gather(phase_delay, "illum", axis=1, tiled=True)
+    all_planes = jnp.concatenate(
+        lax.all_to_all(jnp.stack([phase_delay] * lax.axis_size("illum")), "illum", 0, 0), axis=1
+    )
     stored = []
     for depth_index in range(phase_delay.shape[0]):
         phase_plane = all_planes[depth_index]

time: 430 us -> 416 us (0.967)
  waiting for transfers between devices: 267 us -> 235 us
  starting transfers between devices: 74.6 us -> 87.6 us
    all_gather x1 -> x0, waiting for transfers between devices: 55.3 us -> none  [per_device(): all_planes = lax.all_gather(phase_delay, 'illum', axis=1, tiled=True)]
    all_to_all x0 -> x1, waiting for transfers between devices: none -> 24.2 us  [per_device(): lax.all_to_all(jnp.stack([phase_delay] * lax.axis_size('illum')), 'illum'...]
    all_to_all x0 -> x1, starting transfers between devices: none -> 11.5 us  [per_device(): lax.all_to_all(jnp.stack([phase_delay] * lax.axis_size('illum')), 'illum'...]
    sub x1 -> x2, other arithmetic: 4.14 us -> 12.8 us  [per_device(): adjoint_wave[1] * modulated[0] - adjoint_wave[0] * modulated[1]]
    another operation x9 -> x4, other arithmetic: 5.28 us -> 0.06 us  [propagate(): beside_all = neighbour_sum(exchange_rims(jnp.stack([real_part, imag_part])))]
    another operation x3 -> x2, other arithmetic: 4.85 us -> 0.03 us  [per_device(): jnp.stack([wave_field[0] * cosine - wave_field[1] * sine_part, wave_field...]
where the time goes in v1:
time: 416 us; the launch traced here: 415 us
  waiting for transfers between devices  235 us (56%)
  starting transfers between devices  87.6 us (21%)
  other arithmetic  39.8 us (10%)
  blocking collectives  31.6 us (8%)
  between operations  14.8 us (4%)
  local copies, waits for them, and re-layouts  6.33 us (2%)
    psum x1, waiting for transfers between devices, per_device(): summed = lax.psum(local_grads, 'illum')  170 us
    ppermute x16, starting transfers between devices, with_halo(): before = lax.ppermute(last, axis, up)  55.3 us
    ppermute x16, waiting for transfers between devices, with_halo(): after = lax.ppermute(first, axis, down)  33.6 us
    psum x1, blocking collectives, per_device(): lax.psum(jnp.sum(target * target, axis=(0, 2, 3)), ('row', 'col'))  31.6 us
    all_to_all x1, waiting for transfers between devices, per_device(): lax.all_to_all(jnp.stack([phase_delay] * lax.axis_size('illum')), 'illum'...  24.2 us
    ppermute x16, starting transfers between devices, with_halo(): after = lax.ppermute(first, axis, down)  20.8 us
    sub x2, other arithmetic, per_device(): adjoint_wave[1] * modulated[0] - adjoint_wave[0] * modulated[1]  12.8 us
    all_to_all x1, starting transfers between devices, per_device(): lax.all_to_all(jnp.stack([phase_delay] * lax.axis_size('illum')), 'illum'...  11.5 us
  transfers between devices with their start and end apart: 34, of which 17 were waited for; matrix products, arithmetic and copies ran while one was open for 1% of the time, Pallas kernels for 0%

profile of v1, /device:TPU:2, one launch (start us, length us, event | category | flops | bytes accessed | tf_op | source)
XLA Modules:
  0.0 414.9 jit_solution(8074191509832939042)
XLA Ops:
  6.5 2.0 stack.20
  8.5 11.5 %all-to-all-start = ((f32[16,2,8,1024]{3,2,1,0:T(8,128)}), f32[16,2,8,1024]{3,2,1,0:T(8,128)S(1)}, u32[]{:S(2)}, u32[]{:S(2)}) async-start(f32[16,2,8,1024]{3,2,1,0:T(8,128)} %stack.20), calls=%async_computation | async-start | bytes 2097152 | tf_op jit(solution)/shard_map/all_to_all | solution.py:86
  22.6 24.2 %all-to-all-done = f32[16,2,8,1024]{3,2,1,0:T(8,128)S(1)} async-done(((f32[16,2,8,1024]{3,2,1,0:T(8,128)}), f32[16,2,8,1024]{3,2,1,0:T(8,128)S(1)}, u32[]{:S(2)}, u32[]{:S(2)}) %all-to-all-start) | async-done | bytes 1048608 | tf_op jit(solution)/shard_map/all_to_all | solution.py:86
  46.7 3.8 fusion.47
  50.6 3.5 collective-permute-start.1
  54.1 1.3 collective-permute-start
  55.4 4.2 %collective-permute-done = f32[2,1,1,1024]{3,2,1,0:T(1,128)S(1)} collective-permute-done((f32[2,1,1,1024]{3,2,1,0:T(1,128)S(1)}, f32[2,1,1,1024]{3,2,1,0:T(1,128)S(1)}, u32[]{:S(2)}, u32[]{:S(2)}) %collective-permute-start) | collective-permute-done | bytes 8224 | tf_op jit(solution)/shard_map/ppermute | solution.py:20
  59.7 1.3 collective-permute-start.2
  61.0 3.0 collective-permute-start.3
  64.1 1.0 collective-permute-done.3
  66.2 3.5 collective-permute-start.5
  69.7 1.3 collective-permute-start.4
  71.1 4.2 %collective-permute-done.4 = f32[2,1,1,1024]{3,2,1,0:T(1,128)S(1)} collective-permute-done((f32[2,1,1,1024]{3,2,1,0:T(1,128)S(1)}, f32[2,1,1,1024]{3,2,1,0:T(1,128)S(1)}, u32[]{:S(2)}, u32[]{:S(2)}) %collective-permute-start.4) | collective-permute-done | bytes 8224 | tf_op jit(solution)/shard_map/ppermute | solution.py:20
  75.4 1.3 collective-permute-start.6
  76.7 3.8 collective-permute-start.7
  80.5 1.0 collective-permute-done.7
  82.1 2.1 fusion.44
  84.3 2.0 fusion.43
  86.3 3.2 collective-permute-start.9
  89.5 1.3 collective-permute-start.8
  90.8 4.2 %collective-permute-done.8 = f32[2,1,1,1024]{3,2,1,0:T(1,128)S(1)} collective-permute-done((f32[2,1,1,1024]{3,2,1,0:T(1,128)S(1)}, f32[2,1,1,1024]{3,2,1,0:T(1,128)S(1)}, u32[]{:S(2)}, u32[]{:S(2)}) %collective-permute-start.8) | collective-permute-done | bytes 8224 | tf_op jit(solution)/shard_map/ppermute | solution.py:20
  95.1 1.3 collective-permute-start.10
  96.4 6.0 %collective-permute-start.11 = (f32[2,1,130,1]{3,2,1,0:T(8,128)S(1)}, f32[2,1,130,1]{3,2,1,0:T(8,128)S(1)}, u32[]{:S(2)}, u32[]{:S(2)}) collective-permute-start(f32[2,1,130,1]{3,2,1,0:T(8,128)S(1)} %get-tuple-element.38), channel_id=1, source_target_pairs={{0,1},{1,2},{2,3},{4,5},{5,6},{6,7},{8,9},{9,10},{10,11},{12,13},{... | collective-permute-start | bytes 3128 | tf_op jit(solution)/shard_map/ppermute | solution.py:19
  102.5 1.0 collective-permute-done.11
  105.4 2.2 collective-permute-start.13
  107.6 1.4 collective-permute-start.12
  109.1 4.2 %collective-permute-done.12 = f32[2,1,1,1024]{3,2,1,0:T(1,128)S(1)} collective-permute-done((f32[2,1,1,1024]{3,2,1,0:T(1,128)S(1)}, f32[2,1,1,1024]{3,2,1,0:T(1,128)S(1)}, u32[]{:S(2)}, u32[]{:S(2)}) %collective-permute-start.12) | collective-permute-done | bytes 8224 | tf_op jit(solution)/shard_map/ppermute | solution.py:20
  114.1 1.3 collective-permute-start.14
  115.4 5.7 %collective-permute-start.15 = (f32[2,1,130,1]{3,2,1,0:T(8,128)}, f32[2,1,130,1]{3,2,1,0:T(8,128)S(1)}, u32[]{:S(2)}, u32[]{:S(2)}) collective-permute-start(f32[2,1,130,1]{3,2,1,0:T(8,128)} %get-tuple-element.36), channel_id=1, source_target_pairs={{0,1},{1,2},{2,3},{4,5},{5,6},{6,7},{8,9},{9,10},{10,11},{12,13},{... | collective-permute-start | bytes 3128 | tf_op jit(solution)/shard_map/ppermute | solution.py:19
  121.1 0.9 fusion.2
  122.0 31.6 %psum.14 = f32[1]{0:T(128)} all-reduce(f32[1]{0:T(128)} %bitcast.7), channel_id=1, replica_groups=mesh['illum'=16,'row'=4,'col'=4] {'row','col'}, use_global_device_ids=true, to_apply=%region_1.2 | all-reduce | flops 1 | bytes 8 | tf_op jit(solution)/shard_map/psum | solution.py:81
  154.3 3.2 fusion.15
  157.8 0.8 copy-done.7
  158.8 1.3 collective-permute-start.17
  160.1 1.3 collective-permute-start.16
  161.4 4.2 %collective-permute-done.16 = f32[2,1,1,1024]{3,2,1,0:T(1,128)S(1)} collective-permute-done((f32[2,1,1,1024]{3,2,1,0:T(1,128)S(1)}, f32[2,1,1,1024]{3,2,1,0:T(1,128)S(1)}, u32[]{:S(2)}, u32[]{:S(2)}) %collective-permute-start.16) | collective-permute-done | bytes 8224 | tf_op jit(solution)/shard_map/ppermute | solution.py:20
  165.8 1.3 collective-permute-start.18
  167.1 3.0 collective-permute-start.19
  170.1 1.0 collective-permute-done.19
  172.4 1.6 collective-permute-start.21
  174.0 1.3 collective-permute-start.20
  175.4 4.2 %collective-permute-done.20 = f32[2,1,1,1024]{3,2,1,0:T(1,128)S(1)} collective-permute-done((f32[2,1,1,1024]{3,2,1,0:T(1,128)S(1)}, f32[2,1,1,1024]{3,2,1,0:T(1,128)S(1)}, u32[]{:S(2)}, u32[]{:S(2)}) %collective-permute-start.20) | collective-permute-done | bytes 8224 | tf_op jit(solution)/shard_map/ppermute | solution.py:20
  179.7 1.3 collective-permute-start.22
  181.0 3.2 collective-permute-start.23
  184.2 0.8 collective-permute-done.23
  185.7 2.1 fusion.45
  187.8 2.0 fusion.46
  189.8 1.9 collective-permute-start.25
  191.8 1.3 collective-permute-start.24
  193.1 4.2 %collective-permute-done.24 = f32[2,1,1,1024]{3,2,1,0:T(1,128)S(1)} collective-permute-done((f32[2,1,1,1024]{3,2,1,0:T(1,128)S(1)}, f32[2,1,1,1024]{3,2,1,0:T(1,128)S(1)}, u32[]{:S(2)}, u32[]{:S(2)}) %collective-permute-start.24) | collective-permute-done | bytes 8224 | tf_op jit(solution)/shard_map/ppermute | solution.py:20
  197.4 1.3 collective-permute-start.26
  198.7 5.2 %collective-permute-start.27 = (f32[2,1,130,1]{3,2,1,0:T(8,128)S(1)}, f32[2,1,130,1]{3,2,1,0:T(8,128)S(1)}, u32[]{:S(2)}, u32[]{:S(2)}) collective-permute-start(f32[2,1,130,1]{3,2,1,0:T(8,128)S(1)} %get-tuple-element.30), channel_id=1, source_target_pairs={{0,1},{1,2},{2,3},{4,5},{5,6},{6,7},{8,9},{9,10},{10,11},{12,13},{... | collective-permute-start | bytes 3128 | tf_op jit(solution)/shard_map/ppermute | solution.py:19
  204.0 1.0 collective-permute-done.27
  206.0 2.2 collective-permute-start.29
  208.2 1.3 collective-permute-start.28
  209.5 4.2 %collective-permute-done.28 = f32[2,1,1,1024]{3,2,1,0:T(1,128)S(1)} collective-permute-done((f32[2,1,1,1024]{3,2,1,0:T(1,128)S(1)}, f32[2,1,1,1024]{3,2,1,0:T(1,128)S(1)}, u32[]{:S(2)}, u32[]{:S(2)}) %collective-permute-start.28) | collective-permute-done | bytes 8224 | tf_op jit(solution)/shard_map/ppermute | solution.py:20
  213.8 1.3 collective-permute-start.30
  215.1 5.7 %collective-permute-start.31 = (f32[2,1,130,1]{3,2,1,0:T(8,128)S(1)}, f32[2,1,130,1]{3,2,1,0:T(8,128)S(1)}, u32[]{:S(2)}, u32[]{:S(2)}) collective-permute-start(f32[2,1,130,1]{3,2,1,0:T(8,128)S(1)} %get-tuple-element.28), channel_id=1, source_target_pairs={{0,1},{1,2},{2,3},{4,5},{5,6},{6,7},{8,9},{9,10},{10,11},{12,13},{... | collective-permute-start | bytes 3128 | tf_op jit(solution)/shard_map/ppermute | solution.py:19
  220.9 1.0 collective-permute-done.31
  222.6 6.5 %multiply_subtract_fusion = (f32[1,128,1024]{2,1,0:T(8,128)S(1)}, f32[1,128,1024]{2,1,0:T(8,128)S(1)}, f32[1,128,1024]{2,1,0:T(8,128)S(1)}) fusion(f32[2,1,128,1024]{3,2,1,0:T(8,128)S(1)} %fusion.3, f32[2,1,128,1024]{3,2,1,0:T(8,128)S(1)} %fusion.6, f32[2,16,8,1024]{3,2,0,1:T(8,128)S(1)} %bitcast.200, f32[1024]{0:T(1024)S(1)} %fusion.65, ...), kind=kLoop, calls=%fused_computation.199 | loop fusion | flops 6946816 | bytes 7868928 | tf_op jit(solution)/shard_map/sub | solution.py:107
  229.1 6.3 %fusion.39 = f32[1,128,1024]{2,1,0:T(8,128)S(1)} fusion(f32[2,1,128,1024]{3,2,1,0:T(8,128)S(1)} %fusion.21, f32[2,1,128,1024]{3,2,1,0:T(8,128)S(1)} %fusion.24, f32[2,16,8,1024]{3,2,0,1:T(8,128)S(1)} %bitcast.201, f32[1,128,1024]{2,1,0:T(8,128)S(1)} %get-tuple-element.7, f32[1,128,1024]{2,1,0:T(8,128)S(1)} %get-tuple-element.6, f32[1024]{0:T(1024)S(1)} %fusion.65, ...), kind=kLoop, calls=%fused_computation.166 | loop fusion | flops 5373952 | bytes 4723200 | tf_op jit(solution)/shard_map/sub | solution.py:107
  235.3 1.1 pad_maximum_fusion.92
  236.4 170.1 %all-reduce.2.cloned.1.call-done = f32[2,128,1024]{2,1,0:T(8,128)} async-done(((f32[2,128,1024]{2,1,0:T(8,128)}), f32[2,128,1024]{2,1,0:T(8,128)}) %all-reduce.2.cloned.1.call-update) | async-done | bytes 1048592 | tf_op jit(solution)/shard_map/psum | solution.py:117
  406.5 1.5 constant_dynamic-slice_fusion
  (71 shorter events, 12.3 us)
Async XLA Ops:
  8.5 38.2 %all-to-all-start = ((f32[16,2,8,1024]{3,2,1,0:T(8,128)}), f32[16,2,8,1024]{3,2,1,0:T(8,128)S(1)}, u32[]{:S(2)}, u32[]{:S(2)}) async-start(f32[16,2,8,1024]{3,2,1,0:T(8,128)} %stack.20), calls=%async_computation | async-start | bytes 2097152 | tf_op jit(solution)/shard_map/all_to_all | solution.py:86
  20.0 386.5 %all-reduce.2.cloned.1.call-start = ((), (), s32[]{:S(2)}) async-start(), calls=%async_computation.1 | async-start | bytes 2097152 | tf_op jit(solution)/shard_map/psum | solution.py:117
  20.0 0.7 copy-start.8
  50.6 4.8 %collective-permute-start.1 = (f32[2,1,1,1024]{3,2,1,0:T(1,128)S(1)}, f32[2,1,1,1024]{3,2,1,0:T(1,128)S(1)}, u32[]{:S(2)}, u32[]{:S(2)}) collective-permute-start(f32[2,1,1,1024]{3,2,1,0:T(1,128)S(1)} %get-tuple-element.59), channel_id=1, source_target_pairs={{0,4},{4,8},{8,12},{1,5},{5,9},{9,13},{2,6},{6,10},{10,14},{3,7},{... | collective-permute-start | bytes 24584 | tf_op jit(solution)/shard_map/ppermute | solution.py:19
  54.1 5.5 %collective-permute-start = (f32[2,1,1,1024]{3,2,1,0:T(1,128)S(1)}, f32[2,1,1,1024]{3,2,1,0:T(1,128)S(1)}, u32[]{:S(2)}, u32[]{:S(2)}) collective-permute-start(f32[2,1,1,1024]{3,2,1,0:T(1,128)S(1)} %get-tuple-element.60), channel_id=1, source_target_pairs={{4,0},{8,4},{12,8},{5,1},{9,5},{13,9},{6,2},{10,6},{14,10},{7,3},{... | collective-permute-start | bytes 24584 | tf_op jit(solution)/shard_map/ppermute | solution.py:20
  59.7 4.3 %collective-permute-start.2 = (f32[2,1,130,1]{3,2,1,0:T(8,128)S(1)}, f32[2,1,130,1]{3,2,1,0:T(8,128)S(1)}, u32[]{:S(2)}, u32[]{:S(2)}) collective-permute-start(f32[2,1,130,1]{3,2,1,0:T(8,128)S(1)} %get-tuple-element.41), channel_id=1, source_target_pairs={{1,0},{2,1},{3,2},{5,4},{6,5},{7,6},{9,8},{10,9},{11,10},{13,12},{... | collective-permute-start | bytes 3128 | tf_op jit(solution)/shard_map/ppermute | solution.py:20
  61.0 4.0 collective-permute-start.3
  66.2 4.8 %collective-permute-start.5 = (f32[2,1,1,1024]{3,2,1,0:T(1,128)S(1)}, f32[2,1,1,1024]{3,2,1,0:T(1,128)S(1)}, u32[]{:S(2)}, u32[]{:S(2)}) collective-permute-start(f32[2,1,1,1024]{3,2,1,0:T(1,128)S(1)} %get-tuple-element.57), channel_id=1, source_target_pairs={{0,4},{4,8},{8,12},{1,5},{5,9},{9,13},{2,6},{6,10},{10,14},{3,7},{... | collective-permute-start | bytes 24584 | tf_op jit(solution)/shard_map/ppermute | solution.py:19
  69.7 5.5 %collective-permute-start.4 = (f32[2,1,1,1024]{3,2,1,0:T(1,128)S(1)}, f32[2,1,1,1024]{3,2,1,0:T(1,128)S(1)}, u32[]{:S(2)}, u32[]{:S(2)}) collective-permute-start(f32[2,1,1,1024]{3,2,1,0:T(1,128)S(1)} %get-tuple-element.58), channel_id=1, source_target_pairs={{4,0},{8,4},{12,8},{5,1},{9,5},{13,9},{6,2},{10,6},{14,10},{7,3},{... | collective-permute-start | bytes 24584 | tf_op jit(solution)/shard_map/ppermute | solution.py:20
  75.4 5.1 %collective-permute-start.6 = (f32[2,1,130,1]{3,2,1,0:T(8,128)S(1)}, f32[2,1,130,1]{3,2,1,0:T(8,128)S(1)}, u32[]{:S(2)}, u32[]{:S(2)}) collective-permute-start(f32[2,1,130,1]{3,2,1,0:T(8,128)S(1)} %get-tuple-element.39), channel_id=1, source_target_pairs={{1,0},{2,1},{3,2},{5,4},{6,5},{7,6},{9,8},{10,9},{11,10},{13,12},{... | collective-permute-start | bytes 3128 | tf_op jit(solution)/shard_map/ppermute | solution.py:20
  76.7 4.8 %collective-permute-start.7 = (f32[2,1,130,1]{3,2,1,0:T(8,128)S(1)}, f32[2,1,130,1]{3,2,1,0:T(8,128)S(1)}, u32[]{:S(2)}, u32[]{:S(2)}) collective-permute-start(f32[2,1,130,1]{3,2,1,0:T(8,128)S(1)} %get-tuple-element.40), channel_id=1, source_target_pairs={{0,1},{1,2},{2,3},{4,5},{5,6},{6,7},{8,9},{9,10},{10,11},{12,13},{... | collective-permute-start | bytes 3128 | tf_op jit(solution)/shard_map/ppermute | solution.py:19
  86.3 4.5 %collective-permute-start.9 = (f32[2,1,1,1024]{3,2,1,0:T(1,128)S(1)}, f32[2,1,1,1024]{3,2,1,0:T(1,128)S(1)}, u32[]{:S(2)}, u32[]{:S(2)}) collective-permute-start(f32[2,1,1,1024]{3,2,1,0:T(1,128)S(1)} %get-tuple-element.55), channel_id=1, source_target_pairs={{0,4},{4,8},{8,12},{1,5},{5,9},{9,13},{2,6},{6,10},{10,14},{3,7},{... | collective-permute-start | bytes 24584 | tf_op jit(solution)/shard_map/ppermute | solution.py:19
  89.5 5.5 %collective-permute-start.8 = (f32[2,1,1,1024]{3,2,1,0:T(1,128)S(1)}, f32[2,1,1,1024]{3,2,1,0:T(1,128)S(1)}, u32[]{:S(2)}, u32[]{:S(2)}) collective-permute-start(f32[2,1,1,1024]{3,2,1,0:T(1,128)S(1)} %get-tuple-element.56), channel_id=1, source_target_pairs={{4,0},{8,4},{12,8},{5,1},{9,5},{13,9},{6,2},{10,6},{14,10},{7,3},{... | collective-permute-start | bytes 24584 | tf_op jit(solution)/shard_map/ppermute | solution.py:20
  95.1 7.3 %collective-permute-start.10 = (f32[2,1,130,1]{3,2,1,0:T(8,128)S(1)}, f32[2,1,130,1]{3,2,1,0:T(8,128)S(1)}, u32[]{:S(2)}, u32[]{:S(2)}) collective-permute-start(f32[2,1,130,1]{3,2,1,0:T(8,128)S(1)} %get-tuple-element.37), channel_id=1, source_target_pairs={{1,0},{2,1},{3,2},{5,4},{6,5},{7,6},{9,8},{10,9},{11,10},{13,12},{... | collective-permute-start | bytes 3128 | tf_op jit(solution)/shard_map/ppermute | solution.py:20
  96.4 7.0 %collective-permute-start.11 = (f32[2,1,130,1]{3,2,1,0:T(8,128)S(1)}, f32[2,1,130,1]{3,2,1,0:T(8,128)S(1)}, u32[]{:S(2)}, u32[]{:S(2)}) collective-permute-start(f32[2,1,130,1]{3,2,1,0:T(8,128)S(1)} %get-tuple-element.38), channel_id=1, source_target_pairs={{0,1},{1,2},{2,3},{4,5},{5,6},{6,7},{8,9},{9,10},{10,11},{12,13},{... | collective-permute-start | bytes 3128 | tf_op jit(solution)/shard_map/ppermute | solution.py:19
  104.4 0.8 copy-start.2
  104.4 1.0 copy-start.4
  104.4 8.9 %copy-start = (f32[1,1,128,1024]{3,2,1,0:T(8,128)}, f32[1,1,128,1024]{3,2,1,0:T(8,128)S(1)}, u32[]{:S(2)}) copy-start(f32[1,1,128,1024]{3,2,1,0:T(8,128)S(1)} %get-tuple-element.14) | copy-start | bytes 1572868
  105.4 7.9 %copy-start.1 = (f32[1,1,128,1024]{3,2,1,0:T(8,128)}, f32[1,1,128,1024]{3,2,1,0:T(8,128)S(1)}, u32[]{:S(2)}) copy-start(f32[1,1,128,1024]{3,2,1,0:T(8,128)S(1)} %subtract_multiply_fusion.5) | copy-start | bytes 1572868
  105.4 3.7 collective-permute-start.13
  107.6 13.5 %copy-start.6 = (bf16[2,1,128,1024]{3,2,1,0:T(8,128)(2,1)S(1)}, bf16[2,1,128,1024]{3,2,1,0:T(8,128)(2,1)}, u32[]{:S(2)}) copy-start(bf16[2,1,128,1024]{3,2,1,0:T(8,128)(2,1)} %param.5) | copy-start | bytes 1572868
  107.6 5.7 %collective-permute-start.12 = (f32[2,1,1,1024]{3,2,1,0:T(1,128)S(1)}, f32[2,1,1,1024]{3,2,1,0:T(1,128)S(1)}, u32[]{:S(2)}, u32[]{:S(2)}) collective-permute-start(f32[2,1,1,1024]{3,2,1,0:T(1,128)S(1)} %get-tuple-element.54), channel_id=1, source_target_pairs={{4,0},{8,4},{12,8},{5,1},{9,5},{13,9},{6,2},{10,6},{14,10},{7,3},{... | collective-permute-start | bytes 24584 | tf_op jit(solution)/shard_map/ppermute | solution.py:20
  114.1 40.2 %collective-permute-start.14 = (f32[2,1,130,1]{3,2,1,0:T(8,128)}, f32[2,1,130,1]{3,2,1,0:T(8,128)S(1)}, u32[]{:S(2)}, u32[]{:S(2)}) collective-permute-start(f32[2,1,130,1]{3,2,1,0:T(8,128)} %get-tuple-element.35), channel_id=1, source_target_pairs={{1,0},{2,1},{3,2},{5,4},{6,5},{7,6},{9,8},{10,9},{11,10},{13,12},{... | collective-permute-start | bytes 3128 | tf_op jit(solution)/shard_map/ppermute | solution.py:20
  115.4 38.9 %collective-permute-start.15 = (f32[2,1,130,1]{3,2,1,0:T(8,128)}, f32[2,1,130,1]{3,2,1,0:T(8,128)S(1)}, u32[]{:S(2)}, u32[]{:S(2)}) collective-permute-start(f32[2,1,130,1]{3,2,1,0:T(8,128)} %get-tuple-element.36), channel_id=1, source_target_pairs={{0,1},{1,2},{2,3},{4,5},{5,6},{6,7},{8,9},{9,10},{10,11},{12,13},{... | collective-permute-start | bytes 3128 | tf_op jit(solution)/shard_map/ppermute | solution.py:19
  154.3 3.2 copy-start.3
  154.3 3.2 copy-start.5
  157.6 1.0 copy-start.7
  158.8 2.6 collective-permute-start.17
  160.1 5.5 %collective-permute-start.16 = (f32[2,1,1,1024]{3,2,1,0:T(1,128)S(1)}, f32[2,1,1,1024]{3,2,1,0:T(1,128)S(1)}, u32[]{:S(2)}, u32[]{:S(2)}) collective-permute-start(f32[2,1,1,1024]{3,2,1,0:T(1,128)S(1)} %get-tuple-element.52), channel_id=1, source_target_pairs={{4,0},{8,4},{12,8},{5,1},{9,5},{13,9},{6,2},{10,6},{14,10},{7,3},{... | collective-permute-start | bytes 24584 | tf_op jit(solution)/shard_map/ppermute | solution.py:20
  165.8 4.3 %collective-permute-start.18 = (f32[2,1,130,1]{3,2,1,0:T(8,128)S(1)}, f32[2,1,130,1]{3,2,1,0:T(8,128)S(1)}, u32[]{:S(2)}, u32[]{:S(2)}) collective-permute-start(f32[2,1,130,1]{3,2,1,0:T(8,128)S(1)} %get-tuple-element.33), channel_id=1, source_target_pairs={{1,0},{2,1},{3,2},{5,4},{6,5},{7,6},{9,8},{10,9},{11,10},{13,12},{... | collective-permute-start | bytes 3128 | tf_op jit(solution)/shard_map/ppermute | solution.py:20
  167.1 4.0 collective-permute-start.19
  172.4 3.0 collective-permute-start.21
  174.0 5.5 %collective-permute-start.20 = (f32[2,1,1,1024]{3,2,1,0:T(1,128)S(1)}, f32[2,1,1,1024]{3,2,1,0:T(1,128)S(1)}, u32[]{:S(2)}, u32[]{:S(2)}) collective-permute-start(f32[2,1,1,1024]{3,2,1,0:T(1,128)S(1)} %get-tuple-element.50), channel_id=1, source_target_pairs={{4,0},{8,4},{12,8},{5,1},{9,5},{13,9},{6,2},{10,6},{14,10},{7,3},{... | collective-permute-start | bytes 24584 | tf_op jit(solution)/shard_map/ppermute | solution.py:20
  179.7 4.5 %collective-permute-start.22 = (f32[2,1,130,1]{3,2,1,0:T(8,128)S(1)}, f32[2,1,130,1]{3,2,1,0:T(8,128)S(1)}, u32[]{:S(2)}, u32[]{:S(2)}) collective-permute-start(f32[2,1,130,1]{3,2,1,0:T(8,128)S(1)} %get-tuple-element.31), channel_id=1, source_target_pairs={{1,0},{2,1},{3,2},{5,4},{6,5},{7,6},{9,8},{10,9},{11,10},{13,12},{... | collective-permute-start | bytes 3128 | tf_op jit(solution)/shard_map/ppermute | solution.py:20
  181.0 4.0 collective-permute-start.23
  189.8 3.3 collective-permute-start.25
  191.8 5.5 %collective-permute-start.24 = (f32[2,1,1,1024]{3,2,1,0:T(1,128)S(1)}, f32[2,1,1,1024]{3,2,1,0:T(1,128)S(1)}, u32[]{:S(2)}, u32[]{:S(2)}) collective-permute-start(f32[2,1,1,1024]{3,2,1,0:T(1,128)S(1)} %get-tuple-element.48), channel_id=1, source_target_pairs={{4,0},{8,4},{12,8},{5,1},{9,5},{13,9},{6,2},{10,6},{14,10},{7,3},{... | collective-permute-start | bytes 24584 | tf_op jit(solution)/shard_map/ppermute | solution.py:20
  197.4 6.5 %collective-permute-start.26 = (f32[2,1,130,1]{3,2,1,0:T(8,128)S(1)}, f32[2,1,130,1]{3,2,1,0:T(8,128)S(1)}, u32[]{:S(2)}, u32[]{:S(2)}) collective-permute-start(f32[2,1,130,1]{3,2,1,0:T(8,128)S(1)} %get-tuple-element.29), channel_id=1, source_target_pairs={{1,0},{2,1},{3,2},{5,4},{6,5},{7,6},{9,8},{10,9},{11,10},{13,12},{... | collective-permute-start | bytes 3128 | tf_op jit(solution)/shard_map/ppermute | solution.py:20
  198.7 6.2 %collective-permute-start.27 = (f32[2,1,130,1]{3,2,1,0:T(8,128)S(1)}, f32[2,1,130,1]{3,2,1,0:T(8,128)S(1)}, u32[]{:S(2)}, u32[]{:S(2)}) collective-permute-start(f32[2,1,130,1]{3,2,1,0:T(8,128)S(1)} %get-tuple-element.30), channel_id=1, source_target_pairs={{0,1},{1,2},{2,3},{4,5},{5,6},{6,7},{8,9},{9,10},{10,11},{12,13},{... | collective-permute-start | bytes 3128 | tf_op jit(solution)/shard_map/ppermute | solution.py:19
  206.0 3.6 collective-permute-start.29
  208.2 5.5 %collective-permute-start.28 = (f32[2,1,1,1024]{3,2,1,0:T(1,128)S(1)}, f32[2,1,1,1024]{3,2,1,0:T(1,128)S(1)}, u32[]{:S(2)}, u32[]{:S(2)}) collective-permute-start(f32[2,1,1,1024]{3,2,1,0:T(1,128)S(1)} %get-tuple-element.46), channel_id=1, source_target_pairs={{4,0},{8,4},{12,8},{5,1},{9,5},{13,9},{6,2},{10,6},{14,10},{7,3},{... | collective-permute-start | bytes 24584 | tf_op jit(solution)/shard_map/ppermute | solution.py:20
  213.8 7.1 %collective-permute-start.30 = (f32[2,1,130,1]{3,2,1,0:T(8,128)S(1)}, f32[2,1,130,1]{3,2,1,0:T(8,128)S(1)}, u32[]{:S(2)}, u32[]{:S(2)}) collective-permute-start(f32[2,1,130,1]{3,2,1,0:T(8,128)S(1)} %get-tuple-element.27), channel_id=1, source_target_pairs={{1,0},{2,1},{3,2},{5,4},{6,5},{7,6},{9,8},{10,9},{11,10},{13,12},{... | collective-permute-start | bytes 3128 | tf_op jit(solution)/shard_map/ppermute | solution.py:20
  215.1 6.7 %collective-permute-start.31 = (f32[2,1,130,1]{3,2,1,0:T(8,128)S(1)}, f32[2,1,130,1]{3,2,1,0:T(8,128)S(1)}, u32[]{:S(2)}, u32[]{:S(2)}) collective-permute-start(f32[2,1,130,1]{3,2,1,0:T(8,128)S(1)} %get-tuple-element.28), channel_id=1, source_target_pairs={{0,1},{1,2},{2,3},{4,5},{5,6},{6,7},{8,9},{9,10},{10,11},{12,13},{... | collective-permute-start | bytes 3128 | tf_op jit(solution)/shard_map/ppermute | solution.py:19
Sparse Core Ops, SparseCore 0:
  236.6 169.9 all-reduce.1
